TPU v7x, 32 devices: a whole 2x2x4 slice. The times are simulated.
32 devices in a mesh: blk: 8 (over z, y), slab: 4 (over x, core).
Axes of the slice: x: 2, y: 2, z: 4, core: 2. Of those that a mesh axis runs over, the one named last changes fastest.
Arguments:
- orbitals: bfloat16 [192, 8, 8, 128], P('blk', 'slab'), may hold values from -6 to 6
- energies: bfloat16 [192], P('blk'), may hold values from -2 to -0.5
- trial_potential: float32 [8, 8, 8, 128], P('blk', 'slab'), may hold values from -6 to 6
- local_potential: float32 [8, 8, 128], P('slab'), may hold values from 0 to 1
- beta: float32 [64, 128], P('slab'), may hold values from -1.25 to 1.25
- support: int32 [64, 128], P('slab'), may hold values from 0 to 2047, as said below
- slot_atom: int32 [64], P('slab'), may hold values from 0 to 31, as said below
- dcoef: float32 [32], replicated, may hold values from 1.5 to 3
Outputs:
- response: float32 [8, 8, 8, 128], P('blk', 'slab')
Inputs may be any that keep to these rules, and one draw needn't show every extreme that they name: `support`: on each slab the 16 slots' supports together list every one of its 2048 cells exactly once. `slot_atom`: atom a belongs to slab a // 8; slab k lists each atom of slab k and each atom of slab (k + 1) modulo the slab count exactly once, in an order drawn from the seed.
All inputs are finite; a program needn't handle non-finite values.
Results may differ from a plain program's by a relative error of at most 0.0003.
Values may be sent and summed in bfloat16 or wider, within the bound.
A program may use at most 64 MiB of HBM per device.

v0:
```python
import functools

import jax
import jax.numpy as jnp
from jax import lax
from jax.experimental import pallas as pl
from jax.experimental.pallas import tpu as pltpu
from jax.sharding import PartitionSpec as P

ITERS = 3
MESH = pl.DeviceIdType.MESH


def split2(value):
    high = value.astype(jnp.bfloat16)
    low = (value - high.astype(jnp.float32)).astype(jnp.bfloat16)
    return high, low


def nt_dot(a, b):
    return lax.dot_general(a, b, (((1,), (1,)), ((), ())), preferred_element_type=jnp.float32)


def kernel(
    cfg, orb, eb, slot_atom, pot, locp, beta, support, dcoef, out,
    psi_buf, e_buf, pack, pack_buf, part, part_buf,
    psi32, psit, x0, hinv, state_a, state_b, onehot,
    psi_send, psi_recv, e_sems, pack_send, pack_recv, part_send, part_recv,
):
    n, nb, u, up, planes, gy, gx, atoms = cfg
    half = n // 2
    rows = planes * gy
    nz = n * planes
    d, k = lax.axis_index("blk"), lax.axis_index("slab")
    before = lax.rem(d + nb - 1, nb)
    after = lax.rem(d + 1, nb)

    barrier = pltpu.get_barrier_semaphore()
    for j in range(1, n):
        pl.semaphore_signal(
            barrier, inc=1, device_id=(d, lax.rem(k + j, n)), device_id_type=MESH)

    @pl.when(k >= half)
    def _():
        for j in range(n):
            pl.semaphore_signal(
                barrier, inc=1, device_id=(before, lax.rem(k + j, n)), device_id_type=MESH)

    sub_rows = lax.broadcasted_iota(jnp.int32, (rows, gx), 0)
    sub_cols = lax.broadcasted_iota(jnp.int32, (gx, gx), 0)
    acc = jnp.zeros((4 * rows, gx), jnp.float32)
    for s in range(beta.shape[0]):
        cell = support[s:s + 1, :]
        value = beta[s:s + 1, :]
        b1 = value.astype(jnp.bfloat16).astype(jnp.float32)
        b2 = (value - b1).astype(jnp.bfloat16).astype(jnp.float32)
        b3 = value - b1 - b2
        hit = sub_rows == lax.shift_right_logical(cell, 7)
        atom = jnp.full((1, 1), slot_atom[s], jnp.int32).astype(jnp.float32)
        left = jnp.concatenate(
            [jnp.where(hit, b1, 0.0), jnp.where(hit, b2, 0.0),
             jnp.where(hit, b3, 0.0), jnp.where(hit, atom, 0.0)], axis=0).astype(jnp.bfloat16)
        right = jnp.where(sub_cols == (cell & 127), 1.0, 0.0).astype(jnp.bfloat16)
        acc = acc + nt_dot(left, right)
    pack[0] = pot[...].reshape(rows, gx)
    pack[1] = locp[...].reshape(rows, gx)
    pack[2] = acc[:rows] + acc[rows:2 * rows] + acc[2 * rows:3 * rows]
    pack[3] = acc[3 * rows:]

    pl.semaphore_wait(barrier, n - 1 + half)

    def psi_copy(j):
        to = lax.rem(k + j, n)
        blk_to = lax.select(to >= half, after, d)
        return pltpu.make_async_remote_copy(
            src_ref=orb.at[lax.rem(to, half)], dst_ref=psi_buf.at[j],
            send_sem=psi_send.at[j], recv_sem=psi_recv.at[j],
            device_id=(blk_to, to), device_id_type=MESH)

    psi_local = pltpu.make_async_copy(orb.at[lax.rem(k, half)], psi_buf.at[0], psi_recv.at[0])
    e_local = pltpu.make_async_copy(eb.at[lax.rem(k, half)], e_buf, e_sems.at[1])
    e_copy = pltpu.make_async_remote_copy(
        src_ref=eb.at[lax.rem(k, half)], dst_ref=e_buf, send_sem=e_sems.at[0],
        recv_sem=e_sems.at[1], device_id=(after, k), device_id_type=MESH)

    def pack_copy(j):
        return pltpu.make_async_remote_copy(
            src_ref=pack, dst_ref=pack_buf.at[j],
            send_sem=pack_send.at[j], recv_sem=pack_recv.at[j],
            device_id=(d, lax.rem(k + j, n)), device_id_type=MESH)

    def part_copy(j):
        to = lax.rem(k + j, n)
        return pltpu.make_async_remote_copy(
            src_ref=part.at[to], dst_ref=part_buf.at[j],
            send_sem=part_send.at[j], recv_sem=part_recv.at[j],
            device_id=(d, to), device_id_type=MESH)

    @pl.when(k < half)
    def _():
        psi_local.start()
        e_local.start()

    @pl.when(k >= half)
    def _():
        e_copy.start()
        psi_copy(0).start()

    for j in range(1, n):
        psi_copy(j).start()
    for j in range(1, n):
        pack_copy(j).start()

    pack_buf[0] = pack[...]
    zero = jnp.zeros((gy, up, gx), jnp.float32)
    for ref in (state_a, state_b):
        ref[0] = zero
        ref[nz + 1] = zero
    if up > u:
        psi32[u * rows:, :] = jnp.zeros(((up - u) * rows, gx), jnp.float32)
    strength = dcoef[...]
    strength = jnp.concatenate([strength, strength], axis=1)
    atom_ids = lax.rem(lax.broadcasted_iota(jnp.int32, (2 * atoms, gx), 0), atoms).astype(jnp.float32)

    def project(z, tiles):
        pairs = [split2(tile) for tile in tiles]
        high = jnp.concatenate([p[0] for p in pairs], axis=1)
        low = jnp.concatenate([p[1] for p in pairs], axis=1)
        both = jnp.concatenate([high, low], axis=0)
        return nt_dot(both, onehot[z])

    proj = jnp.zeros((2 * up, 2 * atoms), jnp.float32)
    for j in range(n):
        if j == 0:
            @pl.when(k < half)
            def _():
                psi_local.wait()
                e_local.wait()

            @pl.when(k >= half)
            def _():
                psi_copy(0).wait_recv()
                e_copy.wait_recv()
        else:
            psi_copy(j).wait_recv()
            pack_copy(j).wait_recv()
        slab = lax.rem(k + n - j, n)
        psi32[:u * rows, :] = psi_buf[j].astype(jnp.float32).reshape(u * rows, gx)
        energy = e_buf[...]
        for p in range(planes):
            z = slab * planes + p
            scaled = []
            for y in range(gy):
                row = p * gy + y
                psi = psi32[pl.ds(row, up, stride=rows), :]
                v = pack_buf[j, 0, row:row + 1, :]
                lp = pack_buf[j, 1, row:row + 1, :]
                bv = pack_buf[j, 2, row:row + 1, :]
                at = pack_buf[j, 3, row:row + 1, :]
                inv = 1.0 / (3.0 + lp - energy)
                start = -(v * psi) * inv
                psit[z, y] = psi
                hinv[z, y] = inv
                x0[z, y] = start
                state_a[z + 1, y] = start
                onehot[z, :, y * gx:(y + 1) * gx] = jnp.where(
                    atom_ids == at, 1.0, 0.0).astype(jnp.bfloat16)
                scaled.append(start * bv)
            proj = proj + project(z, scaled)

    lanes = lax.broadcasted_iota(jnp.int32, (up, 2 * atoms), 1)
    for step in range(ITERS):
        src, dst = (state_a, state_b) if step % 2 == 0 else (state_b, state_a)
        last = step == ITERS - 1
        coefs = (proj[:up] + proj[up:]) * strength
        high = coefs.astype(jnp.bfloat16).astype(jnp.float32)
        coefs = jnp.where(lanes < atoms, high, coefs - high).astype(jnp.bfloat16)
        proj = jnp.zeros((2 * up, 2 * atoms), jnp.float32)
        for j in range(n):
            slab = lax.rem(k + n - j, n)
            for p in range(planes):
                z = slab * planes + p
                back = jnp.dot(coefs, onehot[z], preferred_element_type=jnp.float32)
                scaled, sums = [], []
                for y in range(gy):
                    row = p * gy + y
                    bv = pack_buf[j, 2, row:row + 1, :]
                    old = src[z + 1, y]
                    near = (src[z, y] + src[z + 2, y]
                            + src[z + 1, (y + 1) % gy] + src[z + 1, (y - 1) % gy]
                            + pltpu.roll(old, 1, 1) + pltpu.roll(old, gx - 1, 1))
                    change = 0.25 * near - (0.5 * bv) * back[:, y * gx:(y + 1) * gx]
                    new = 0.5 * (old + x0[z, y]) + hinv[z, y] * change
                    if last:
                        sums.append(jnp.sum(psit[z, y] * new, axis=0, keepdims=True))
                    else:
                        dst[z + 1, y] = new
                        scaled.append(new * bv)
                if last:
                    part[slab, p * gy:(p + 1) * gy, :] = jnp.concatenate(sums, axis=0)
                else:
                    proj = proj + project(z, scaled)

    for j in range(1, n):
        part_copy(j).start()
    total = part[k]
    for j in range(1, n):
        part_copy(j).wait_recv()
        total = total + part_buf[j]
    out[...] = total.reshape(out.shape)

    for j in range(1, n):
        psi_copy(j).wait_send()
        pack_copy(j).wait_send()
        part_copy(j).wait_send()

    @pl.when(k >= half)
    def _():
        psi_copy(0).wait_send()
        e_copy.wait_send()


def shards(orbitals, energies, trial_potential, local_potential, beta, support, slot_atom, dcoef):
    n, nb = lax.axis_size("slab"), lax.axis_size("blk")
    count, planes, gy, gx = orbitals.shape
    half = n // 2
    u = count // half
    up = -(-u // 16) * 16
    atoms = dcoef.shape[0]
    nz, rows = n * planes, planes * gy
    orb = orbitals.reshape(half, u, planes, gy, gx)
    eb = jnp.pad(energies.astype(jnp.float32).reshape(half, u), ((0, 0), (0, up - u)),
                 constant_values=-1.0)
    eb = jnp.broadcast_to(eb[:, :, None], (half, up, gx))
    f32, bf16 = jnp.float32, jnp.bfloat16
    vmem = pl.BlockSpec(memory_space=pltpu.VMEM)
    hbm = pl.BlockSpec(memory_space=pl.ANY)
    dma = pltpu.SemaphoreType.DMA
    return pl.pallas_call(
        functools.partial(kernel, (n, nb, u, up, planes, gy, gx, atoms)),
        out_shape=jax.ShapeDtypeStruct(trial_potential.shape, f32),
        in_specs=[hbm, vmem, pl.BlockSpec(memory_space=pltpu.SMEM), vmem, vmem, vmem, vmem, vmem],
        out_specs=vmem,
        scratch_shapes=[
            pltpu.VMEM((n, u, planes, gy, gx), bf16),
            pltpu.VMEM((up, gx), f32),
            pltpu.VMEM((4, rows, gx), f32),
            pltpu.VMEM((n, 4, rows, gx), f32),
            pltpu.VMEM((n, rows, gx), f32),
            pltpu.VMEM((n, rows, gx), f32),
            pltpu.VMEM((up * rows, gx), f32),
            pltpu.VMEM((nz, gy, up, gx), f32),
            pltpu.VMEM((nz, gy, up, gx), f32),
            pltpu.VMEM((nz, gy, up, gx), f32),
            pltpu.VMEM((nz + 2, gy, up, gx), f32),
            pltpu.VMEM((nz + 2, gy, up, gx), f32),
            pltpu.VMEM((nz, 2 * atoms, gy * gx), bf16),
            dma((n,)), dma((n,)), dma((2,)), dma((n,)), dma((n,)), dma((n,)), dma((n,)),
        ],
        compiler_params=pltpu.CompilerParams(
            collective_id=0, has_side_effects=True, vmem_limit_bytes=48 << 20),
    )(orb, eb, slot_atom, trial_potential, local_potential, beta, support, dcoef.reshape(1, atoms))


def solution(mesh):
    placed = (
        P("blk", "slab", None, None),
        P("blk"),
        P("blk", "slab", None, None),
        P("slab", None, None),
        P("slab", None),
        P("slab", None),
        P("slab"),
        P(),
    )
    return jax.shard_map(
        shards, mesh=mesh, in_specs=placed, out_specs=P("blk", "slab", None, None), check_vma=False
    )
```

profile of v0, /device:TPU:0, one launch (start us, length us, event | category | flops | bytes accessed | tf_op | source)
XLA Modules:
  0.0 22.7 jit_solution(4034001016791938681)
XLA Ops:
  0.0 0.0 copy-start.3
  0.0 0.8 %reshape.12 = bf16[2,12]{1,0:T(2,128)(2,1)S(1)} reshape(bf16[24]{0:T(256)(128)(2,1)} %param.9) | data formatting | bytes 96 | tf_op jit(solution)/shard_map/reshape | solution.py:232
  0.8 0.0 copy-start.1
  0.8 0.0 copy-start.2
  0.8 0.0 copy-start.5
  0.8 0.1 broadcast_in_dim.2.eb
  0.9 0.0 copy-done.3
  0.9 0.6 %copy-done.1 = f32[1,2,8,128]{3,2,1,0:T(8,128)S(1)} copy-done((f32[1,2,8,128]{3,2,1,0:T(8,128)S(1)}, f32[1,2,8,128]{3,2,1,0:T(8,128)}, u32[]{:S(2)}) %copy-start.1) | copy-done | bytes 8216
  1.5 0.0 copy-done.2
  1.5 0.0 copy-done.5
  1.5 0.0 copy-start
  1.5 0.9 %copy-done = bf16[24,2,8,128]{3,2,1,0:T(8,128)(2,1)S(1)} copy-done((bf16[24,2,8,128]{3,2,1,0:T(8,128)(2,1)S(1)}, bf16[24,2,8,128]{3,2,1,0:T(8,128)(2,1)}, u32[]{:S(2)}) %copy-start) | copy-done | bytes 98328
  2.4 0.0 copy-start.4
  2.4 0.7 %copy-done.4 = s32[16,128]{1,0:T(8,128)S(1)} copy-done((s32[16,128]{1,0:T(8,128)S(1)}, s32[16,128]{1,0:T(8,128)}, u32[]{:S(2)}) %copy-start.4) | copy-done | bytes 8216
  3.1 0.0 copy-start.6
  3.1 0.7 %copy-done.6 = f32[32]{0:T(128)S(1)} copy-done((f32[32]{0:T(128)S(1)}, f32[32]{0:T(128)}, u32[]{:S(2)}) %copy-start.6) | copy-done | bytes 152
  3.7 18.3 %shard_map.82 = f32[1,2,8,128]{3,2,1,0:T(8,128)S(1)} custom-call(bf16[2,12,2,8,128]{4,3,2,1,0:T(8,128)(2,1)S(1)} %bitcast.2, f32[2,16,128]{2,1,0:T(8,128)S(1)} %broadcast_in_dim.2.eb, s32[16]{0:T(128)S(1)} %copy-done.5, f32[1,2,8,128]{3,2,1,0:T(8,128)S(1)} %copy-done.1, f32[2,8,128]{2,1,0:T(8,128)S(1)} %copy-done.2, f32[16,128]{1,0:T(8,128)S(1)} %copy-done.3, ...), custom_call_target="tpu_custom_call" | custom-call | tf_op jit(solution)/shard_map/pallas_call | solution.py:239
  22.1 0.6 %copy.10 = f32[1,2,8,128]{3,2,1,0:T(8,128)} copy(f32[1,2,8,128]{3,2,1,0:T(8,128)S(1)} %shard_map.82) | data formatting | bytes 16384
  (1 shorter events, 0.0 us)
Async XLA Ops:
  0.0 0.9 %copy-start.3 = (f32[16,128]{1,0:T(8,128)S(1)}, f32[16,128]{1,0:T(8,128)}, u32[]{:S(2)}) copy-start(f32[16,128]{1,0:T(8,128)} %beta.1) | copy-start | bytes 24580
  0.8 0.7 %copy-start.1 = (f32[1,2,8,128]{3,2,1,0:T(8,128)S(1)}, f32[1,2,8,128]{3,2,1,0:T(8,128)}, u32[]{:S(2)}) copy-start(f32[1,2,8,128]{3,2,1,0:T(8,128)} %pot.1) | copy-start | bytes 24580
  0.8 0.7 %copy-start.2 = (f32[2,8,128]{2,1,0:T(8,128)S(1)}, f32[2,8,128]{2,1,0:T(8,128)}, u32[]{:S(2)}) copy-start(f32[2,8,128]{2,1,0:T(8,128)} %locp.1) | copy-start | bytes 24580
  0.8 0.7 %copy-start.5 = (s32[16]{0:T(128)S(1)}, s32[16]{0:T(128)}, u32[]{:S(2)}) copy-start(s32[16]{0:T(128)} %slot_atom.1) | copy-start | bytes 196
  1.5 0.9 %copy-start = (bf16[24,2,8,128]{3,2,1,0:T(8,128)(2,1)S(1)}, bf16[24,2,8,128]{3,2,1,0:T(8,128)(2,1)}, u32[]{:S(2)}) copy-start(bf16[24,2,8,128]{3,2,1,0:T(8,128)(2,1)} %param.8) | copy-start | bytes 294916
  2.4 0.7 %copy-start.4 = (s32[16,128]{1,0:T(8,128)S(1)}, s32[16,128]{1,0:T(8,128)}, u32[]{:S(2)}) copy-start(s32[16,128]{1,0:T(8,128)} %support.1) | copy-start | bytes 24580
  3.1 0.7 %copy-start.6 = (f32[32]{0:T(128)S(1)}, f32[32]{0:T(128)}, u32[]{:S(2)}) copy-start(f32[32]{0:T(128)} %param.15) | copy-start | bytes 388
where the time goes:
time: 23 us; the launch traced here: 22.7 us
  Pallas kernels  18.3 us (80%)
  local copies, waits for them, and re-layouts  4.3 us (19%)
    pallas_call x1, Pallas kernels, shards(): pl.pallas_call(functools.partial(kernel, (n, nb, u, up, planes, gy, gx, a...  18.3 us
    unnamed x15, local copies, waits for them, and re-layouts  3.48 us
    reshape x1, local copies, waits for them, and re-layouts, shards(): energies.astype(jnp.float32).reshape(half, u)  0.75 us

commit v1 on v0

--- a/solution.py
+++ b/solution.py
@@ -22,10 +22,10 @@
 
 
 def kernel(
-    cfg, orb, eb, slot_atom, pot, locp, beta, support, dcoef, out,
-    psi_buf, e_buf, pack, pack_buf, part, part_buf,
+    cfg, orb, eng, slot_atom_in, pot, locp, beta_in, support_in, dcoef_in, out,
+    psi_buf, e_buf, slot_atom, beta, support, dcoef, pack_buf, part, part_buf,
     psi32, psit, x0, hinv, state_a, state_b, onehot,
-    psi_send, psi_recv, e_sems, pack_send, pack_recv, part_send, part_recv,
+    psi_send, psi_recv, e_sems, in_sems, pack_send, pack_recv, part_send, part_recv,
 ):
     n, nb, u, up, planes, gy, gx, atoms = cfg
     half = n // 2
@@ -35,6 +35,13 @@
     before = lax.rem(d + nb - 1, nb)
     after = lax.rem(d + 1, nb)
 
+    loads = [
+        pltpu.make_async_copy(src, dst, in_sems.at[i]) for i, (src, dst) in enumerate((
+            (support_in, support), (beta_in, beta), (slot_atom_in, slot_atom),
+            (dcoef_in, dcoef), (pot.at[0], pack_buf.at[k, 0]), (locp, pack_buf.at[k, 1])))]
+    for load in loads:
+        load.start()
+
     barrier = pltpu.get_barrier_semaphore()
     for j in range(1, n):
         pl.semaphore_signal(
@@ -46,9 +53,52 @@
             pl.semaphore_signal(
                 barrier, inc=1, device_id=(before, lax.rem(k + j, n)), device_id_type=MESH)
 
+    pl.semaphore_wait(barrier, n - 1 + half)
+
+    def psi_copy(j):
+        to = lax.rem(k + j, n)
+        blk_to = lax.select(to >= half, after, d)
+        return pltpu.make_async_remote_copy(
+            src_ref=orb.at[lax.rem(to, half)], dst_ref=psi_buf.at[j],
+            send_sem=psi_send.at[j], recv_sem=psi_recv.at[j],
+            device_id=(blk_to, to), device_id_type=MESH)
+
+    psi_local = pltpu.make_async_copy(orb.at[lax.rem(k, half)], psi_buf.at[0], psi_recv.at[0])
+    e_local = pltpu.make_async_copy(eng, e_buf, e_sems.at[1])
+    e_copy = pltpu.make_async_remote_copy(
+        src_ref=eng, dst_ref=e_buf, send_sem=e_sems.at[0],
+        recv_sem=e_sems.at[1], device_id=(after, k), device_id_type=MESH)
+
+    def pack_copy(j):
+        return pltpu.make_async_remote_copy(
+            src_ref=pack_buf.at[k], dst_ref=pack_buf.at[k],
+            send_sem=pack_send.at[j], recv_sem=pack_recv.at[j],
+            device_id=(d, lax.rem(k + j, n)), device_id_type=MESH)
+
+    def part_copy(j):
+        to = lax.rem(k + j, n)
+        return pltpu.make_async_remote_copy(
+            src_ref=part.at[to], dst_ref=part_buf.at[j],
+            send_sem=part_send.at[j], recv_sem=part_recv.at[j],
+            device_id=(d, to), device_id_type=MESH)
+
+    @pl.when(k < half)
+    def _():
+        psi_local.start()
+        e_local.start()
+
+    @pl.when(k >= half)
+    def _():
+        e_copy.start()
+        psi_copy(0).start()
+
+    for j in range(1, n):
+        psi_copy(j).start()
+    for load in loads:
+        load.wait()
     sub_rows = lax.broadcasted_iota(jnp.int32, (rows, gx), 0)
     sub_cols = lax.broadcasted_iota(jnp.int32, (gx, gx), 0)
-    acc = jnp.zeros((4 * rows, gx), jnp.float32)
+    lefts, rights = [], []
     for s in range(beta.shape[0]):
         cell = support[s:s + 1, :]
         value = beta[s:s + 1, :]
@@ -57,61 +107,18 @@
         b3 = value - b1 - b2
         hit = sub_rows == lax.shift_right_logical(cell, 7)
         atom = jnp.full((1, 1), slot_atom[s], jnp.int32).astype(jnp.float32)
-        left = jnp.concatenate(
+        lefts.append(jnp.concatenate(
             [jnp.where(hit, b1, 0.0), jnp.where(hit, b2, 0.0),
-             jnp.where(hit, b3, 0.0), jnp.where(hit, atom, 0.0)], axis=0).astype(jnp.bfloat16)
-        right = jnp.where(sub_cols == (cell & 127), 1.0, 0.0).astype(jnp.bfloat16)
-        acc = acc + nt_dot(left, right)
-    pack[0] = pot[...].reshape(rows, gx)
-    pack[1] = locp[...].reshape(rows, gx)
-    pack[2] = acc[:rows] + acc[rows:2 * rows] + acc[2 * rows:3 * rows]
-    pack[3] = acc[3 * rows:]
-
-    pl.semaphore_wait(barrier, n - 1 + half)
-
-    def psi_copy(j):
-        to = lax.rem(k + j, n)
-        blk_to = lax.select(to >= half, after, d)
-        return pltpu.make_async_remote_copy(
-            src_ref=orb.at[lax.rem(to, half)], dst_ref=psi_buf.at[j],
-            send_sem=psi_send.at[j], recv_sem=psi_recv.at[j],
-            device_id=(blk_to, to), device_id_type=MESH)
-
-    psi_local = pltpu.make_async_copy(orb.at[lax.rem(k, half)], psi_buf.at[0], psi_recv.at[0])
-    e_local = pltpu.make_async_copy(eb.at[lax.rem(k, half)], e_buf, e_sems.at[1])
-    e_copy = pltpu.make_async_remote_copy(
-        src_ref=eb.at[lax.rem(k, half)], dst_ref=e_buf, send_sem=e_sems.at[0],
-        recv_sem=e_sems.at[1], device_id=(after, k), device_id_type=MESH)
-
-    def pack_copy(j):
-        return pltpu.make_async_remote_copy(
-            src_ref=pack, dst_ref=pack_buf.at[j],
-            send_sem=pack_send.at[j], recv_sem=pack_recv.at[j],
-            device_id=(d, lax.rem(k + j, n)), device_id_type=MESH)
-
-    def part_copy(j):
-        to = lax.rem(k + j, n)
-        return pltpu.make_async_remote_copy(
-            src_ref=part.at[to], dst_ref=part_buf.at[j],
-            send_sem=part_send.at[j], recv_sem=part_recv.at[j],
-            device_id=(d, to), device_id_type=MESH)
-
-    @pl.when(k < half)
-    def _():
-        psi_local.start()
-        e_local.start()
-
-    @pl.when(k >= half)
-    def _():
-        e_copy.start()
-        psi_copy(0).start()
-
-    for j in range(1, n):
-        psi_copy(j).start()
+             jnp.where(hit, b3, 0.0), jnp.where(hit, atom, 0.0)], axis=0).astype(jnp.bfloat16))
+        rights.append(jnp.where(sub_cols == (cell & 127), 1.0, 0.0).astype(jnp.bfloat16))
+    acc = nt_dot(jnp.concatenate(lefts, axis=1), jnp.concatenate(rights, axis=1))
+    cellwise = acc[:rows] + acc[rows:2 * rows] + acc[2 * rows:3 * rows]
+    pack_buf[k, 2] = cellwise.reshape(planes, gy, gx)
+    pack_buf[k, 3] = acc[3 * rows:].reshape(planes, gy, gx)
+
     for j in range(1, n):
         pack_copy(j).start()
 
-    pack_buf[0] = pack[...]
     zero = jnp.zeros((gy, up, gx), jnp.float32)
     for ref in (state_a, state_b):
         ref[0] = zero
@@ -146,17 +153,22 @@
             pack_copy(j).wait_recv()
         slab = lax.rem(k + n - j, n)
         psi32[:u * rows, :] = psi_buf[j].astype(jnp.float32).reshape(u * rows, gx)
-        energy = e_buf[...]
+        if j == 0:
+            held = e_buf[...].astype(jnp.float32).reshape(1, u * half)
+            wanted = lax.broadcasted_iota(jnp.int32, (up, u * half), 0) + u * lax.rem(k, half)
+            own = wanted == lax.broadcasted_iota(jnp.int32, (up, u * half), 1)
+            energy = jnp.broadcast_to(
+                jnp.sum(jnp.where(own, held, 0.0), axis=1, keepdims=True), (up, gx))
         for p in range(planes):
             z = slab * planes + p
             scaled = []
             for y in range(gy):
                 row = p * gy + y
                 psi = psi32[pl.ds(row, up, stride=rows), :]
-                v = pack_buf[j, 0, row:row + 1, :]
-                lp = pack_buf[j, 1, row:row + 1, :]
-                bv = pack_buf[j, 2, row:row + 1, :]
-                at = pack_buf[j, 3, row:row + 1, :]
+                v = pack_buf[slab, 0, p, y:y + 1, :]
+                lp = pack_buf[slab, 1, p, y:y + 1, :]
+                bv = pack_buf[slab, 2, p, y:y + 1, :]
+                at = pack_buf[slab, 3, p, y:y + 1, :]
                 inv = 1.0 / (3.0 + lp - energy)
                 start = -(v * psi) * inv
                 psit[z, y] = psi
@@ -176,15 +188,13 @@
         high = coefs.astype(jnp.bfloat16).astype(jnp.float32)
         coefs = jnp.where(lanes < atoms, high, coefs - high).astype(jnp.bfloat16)
         proj = jnp.zeros((2 * up, 2 * atoms), jnp.float32)
-        for j in range(n):
-            slab = lax.rem(k + n - j, n)
+        for slab in range(n):
             for p in range(planes):
                 z = slab * planes + p
                 back = jnp.dot(coefs, onehot[z], preferred_element_type=jnp.float32)
                 scaled, sums = [], []
                 for y in range(gy):
-                    row = p * gy + y
-                    bv = pack_buf[j, 2, row:row + 1, :]
+                    bv = pack_buf[slab, 2, p, y:y + 1, :]
                     old = src[z + 1, y]
                     near = (src[z, y] + src[z + 2, y]
                             + src[z + 1, (y + 1) % gy] + src[z + 1, (y - 1) % gy]
@@ -229,23 +239,23 @@
     atoms = dcoef.shape[0]
     nz, rows = n * planes, planes * gy
     orb = orbitals.reshape(half, u, planes, gy, gx)
-    eb = jnp.pad(energies.astype(jnp.float32).reshape(half, u), ((0, 0), (0, up - u)),
-                 constant_values=-1.0)
-    eb = jnp.broadcast_to(eb[:, :, None], (half, up, gx))
     f32, bf16 = jnp.float32, jnp.bfloat16
     vmem = pl.BlockSpec(memory_space=pltpu.VMEM)
-    hbm = pl.BlockSpec(memory_space=pl.ANY)
+    hbm = pl.BlockSpec(memory_space=pltpu.HBM)
     dma = pltpu.SemaphoreType.DMA
     return pl.pallas_call(
         functools.partial(kernel, (n, nb, u, up, planes, gy, gx, atoms)),
         out_shape=jax.ShapeDtypeStruct(trial_potential.shape, f32),
-        in_specs=[hbm, vmem, pl.BlockSpec(memory_space=pltpu.SMEM), vmem, vmem, vmem, vmem, vmem],
+        in_specs=[hbm] * 8,
         out_specs=vmem,
         scratch_shapes=[
             pltpu.VMEM((n, u, planes, gy, gx), bf16),
-            pltpu.VMEM((up, gx), f32),
-            pltpu.VMEM((4, rows, gx), f32),
-            pltpu.VMEM((n, 4, rows, gx), f32),
+            pltpu.VMEM(energies.shape, bf16),
+            pltpu.SMEM(slot_atom.shape, jnp.int32),
+            pltpu.VMEM(beta.shape, f32),
+            pltpu.VMEM(support.shape, jnp.int32),
+            pltpu.VMEM((1, atoms), f32),
+            pltpu.VMEM((n, 4, planes, gy, gx), f32),
             pltpu.VMEM((n, rows, gx), f32),
             pltpu.VMEM((n, rows, gx), f32),
             pltpu.VMEM((up * rows, gx), f32),
@@ -255,11 +265,11 @@
             pltpu.VMEM((nz + 2, gy, up, gx), f32),
             pltpu.VMEM((nz + 2, gy, up, gx), f32),
             pltpu.VMEM((nz, 2 * atoms, gy * gx), bf16),
-            dma((n,)), dma((n,)), dma((2,)), dma((n,)), dma((n,)), dma((n,)), dma((n,)),
+            dma((n,)), dma((n,)), dma((2,)), dma((6,)), dma((n,)), dma((n,)), dma((n,)), dma((n,)),
         ],
         compiler_params=pltpu.CompilerParams(
-            collective_id=0, has_side_effects=True, vmem_limit_bytes=48 << 20),
-    )(orb, eb, slot_atom, trial_potential, local_potential, beta, support, dcoef.reshape(1, atoms))
+            collective_id=0, has_side_effects=True, vmem_limit_bytes=60 << 20),
+    )(orb, energies, slot_atom, trial_potential, local_potential, beta, support, dcoef.reshape(1, atoms))
 
 
 def solution(mesh):

time: 23 us -> 19.9 us (0.87)
  local copies, waits for them, and re-layouts: 4.3 us -> 1.3 us
    unnamed x15 -> x1, local copies, waits for them, and re-layouts: 3.48 us -> 1.3 us
    reshape x1 -> x0, local copies, waits for them, and re-layouts: 0.75 us -> none  [shards(): energies.astype(jnp.float32).reshape(half, u)]
where the time goes in v1:
time: 19.9 us; the launch traced here: 19.6 us
  Pallas kernels  18.3 us (92%)
  local copies, waits for them, and re-layouts  1.3 us (7%)
    pallas_call x1, Pallas kernels, shards(): pl.pallas_call(functools.partial(kernel, (n, nb, u, up, planes, gy, gx, a...  18.3 us
    unnamed x1, local copies, waits for them, and re-layouts  1.3 us

profile of v1, /device:TPU:0, one launch (start us, length us, event | category | flops | bytes accessed | tf_op | source)
XLA Modules:
  0.0 19.6 jit_solution(17984858791298018942)
XLA Ops:
  0.0 18.3 %shard_map.82 = f32[1,2,8,128]{3,2,1,0:T(8,128)} custom-call(bf16[2,12,2,8,128]{4,3,2,1,0:T(8,128)(2,1)} %bitcast.2, bf16[24]{0:T(256)(128)(2,1)} %eng.1, s32[16]{0:T(128)} %slot_atom_in.1, f32[1,2,8,128]{3,2,1,0:T(8,128)} %pot.1, f32[2,8,128]{2,1,0:T(8,128)} %locp.1, f32[16,128]{1,0:T(8,128)} %beta_in.1, s32[16,128]{1,0:T(8,128)} %support_in.1, f32[1,32]{1,0:T(1,128)} %bitcast.3), custom_call_target="tpu_custom_call" | custom-call | tf_op jit(solution)/shard_map/pallas_call | solution.py:246
  18.3 1.3 %copy.10 = f32[1,2,8,128]{3,2,1,0:T(8,128)} copy(f32[1,2,8,128]{3,2,1,0:T(8,128)} %shard_map.82) | data formatting | bytes 16384

commit v2 on v1

--- a/solution.py
+++ b/solution.py
@@ -32,6 +32,7 @@
     rows = planes * gy
     nz = n * planes
     d, k = lax.axis_index("blk"), lax.axis_index("slab")
+    takes_prior = lax.rem(k, 2) == 1
     before = lax.rem(d + nb - 1, nb)
     after = lax.rem(d + 1, nb)
 
@@ -47,7 +48,7 @@
         pl.semaphore_signal(
             barrier, inc=1, device_id=(d, lax.rem(k + j, n)), device_id_type=MESH)
 
-    @pl.when(k >= half)
+    @pl.when(takes_prior)
     def _():
         for j in range(n):
             pl.semaphore_signal(
@@ -57,13 +58,13 @@
 
     def psi_copy(j):
         to = lax.rem(k + j, n)
-        blk_to = lax.select(to >= half, after, d)
+        blk_to = lax.select(lax.rem(to, 2) == 1, after, d)
         return pltpu.make_async_remote_copy(
-            src_ref=orb.at[lax.rem(to, half)], dst_ref=psi_buf.at[j],
+            src_ref=orb.at[lax.div(to, 2)], dst_ref=psi_buf.at[j],
             send_sem=psi_send.at[j], recv_sem=psi_recv.at[j],
             device_id=(blk_to, to), device_id_type=MESH)
 
-    psi_local = pltpu.make_async_copy(orb.at[lax.rem(k, half)], psi_buf.at[0], psi_recv.at[0])
+    psi_local = pltpu.make_async_copy(orb.at[lax.div(k, 2)], psi_buf.at[0], psi_recv.at[0])
     e_local = pltpu.make_async_copy(eng, e_buf, e_sems.at[1])
     e_copy = pltpu.make_async_remote_copy(
         src_ref=eng, dst_ref=e_buf, send_sem=e_sems.at[0],
@@ -82,12 +83,12 @@
             send_sem=part_send.at[j], recv_sem=part_recv.at[j],
             device_id=(d, to), device_id_type=MESH)
 
-    @pl.when(k < half)
+    @pl.when(jnp.logical_not(takes_prior))
     def _():
         psi_local.start()
         e_local.start()
 
-    @pl.when(k >= half)
+    @pl.when(takes_prior)
     def _():
         e_copy.start()
         psi_copy(0).start()
@@ -139,12 +140,12 @@
     proj = jnp.zeros((2 * up, 2 * atoms), jnp.float32)
     for j in range(n):
         if j == 0:
-            @pl.when(k < half)
+            @pl.when(jnp.logical_not(takes_prior))
             def _():
                 psi_local.wait()
                 e_local.wait()
 
-            @pl.when(k >= half)
+            @pl.when(takes_prior)
             def _():
                 psi_copy(0).wait_recv()
                 e_copy.wait_recv()
@@ -155,7 +156,7 @@
         psi32[:u * rows, :] = psi_buf[j].astype(jnp.float32).reshape(u * rows, gx)
         if j == 0:
             held = e_buf[...].astype(jnp.float32).reshape(1, u * half)
-            wanted = lax.broadcasted_iota(jnp.int32, (up, u * half), 0) + u * lax.rem(k, half)
+            wanted = lax.broadcasted_iota(jnp.int32, (up, u * half), 0) + u * lax.div(k, 2)
             own = wanted == lax.broadcasted_iota(jnp.int32, (up, u * half), 1)
             energy = jnp.broadcast_to(
                 jnp.sum(jnp.where(own, held, 0.0), axis=1, keepdims=True), (up, gx))
@@ -188,7 +189,8 @@
         high = coefs.astype(jnp.bfloat16).astype(jnp.float32)
         coefs = jnp.where(lanes < atoms, high, coefs - high).astype(jnp.bfloat16)
         proj = jnp.zeros((2 * up, 2 * atoms), jnp.float32)
-        for slab in range(n):
+        for j in list(range(1, n)) + [0]:
+            slab = lax.rem(k + j, n) if last else j
             for p in range(planes):
                 z = slab * planes + p
                 back = jnp.dot(coefs, onehot[z], preferred_element_type=jnp.float32)
@@ -210,9 +212,9 @@
                     part[slab, p * gy:(p + 1) * gy, :] = jnp.concatenate(sums, axis=0)
                 else:
                     proj = proj + project(z, scaled)
-
-    for j in range(1, n):
-        part_copy(j).start()
+            if last and j > 0:
+                part_copy(j).start()
+
     total = part[k]
     for j in range(1, n):
         part_copy(j).wait_recv()
@@ -224,7 +226,7 @@
         pack_copy(j).wait_send()
         part_copy(j).wait_send()
 
-    @pl.when(k >= half)
+    @pl.when(takes_prior)
     def _():
         psi_copy(0).wait_send()
         e_copy.wait_send()
@@ -268,8 +270,10 @@
             dma((n,)), dma((n,)), dma((2,)), dma((6,)), dma((n,)), dma((n,)), dma((n,)), dma((n,)),
         ],
         compiler_params=pltpu.CompilerParams(
-            collective_id=0, has_side_effects=True, vmem_limit_bytes=60 << 20),
-    )(orb, energies, slot_atom, trial_potential, local_potential, beta, support, dcoef.reshape(1, atoms))
+            collective_id=0, has_side_effects=True, vmem_limit_bytes=32 << 20),
+    )(*[pltpu.with_memory_space_constraint(a, pltpu.HBM) for a in (
+        orb, energies, slot_atom, trial_potential, local_potential, beta, support,
+        dcoef.reshape(1, atoms))])
 
 
 def solution(mesh):

time: 19.9 us -> 16.6 us (0.83)
  Pallas kernels: 18.3 us -> 15.8 us
  local copies, waits for them, and re-layouts: 1.3 us -> 0.6 us
    pallas_call x1, Pallas kernels: 18.3 us -> 15.8 us  [shards(): pl.pallas_call(functools.partial(kernel, (n, nb, u, up, planes, gy, gx, a...]
    unnamed x1, local copies, waits for them, and re-layouts: 1.3 us -> 0.6 us
where the time goes in v2:
time: 16.6 us; the launch traced here: 16.4 us
  Pallas kernels  15.8 us (95%)
  local copies, waits for them, and re-layouts  0.6 us (4%)
    pallas_call x1, Pallas kernels, shards(): pl.pallas_call(functools.partial(kernel, (n, nb, u, up, planes, gy, gx, a...  15.8 us
    unnamed x1, local copies, waits for them, and re-layouts  0.6 us

profile of v2, /device:TPU:0, one launch (start us, length us, event | category | flops | bytes accessed | tf_op | source)
XLA Modules:
  0.0 16.4 jit_solution(5086128311540114574)
XLA Ops:
  0.0 15.8 %shard_map.82 = f32[1,2,8,128]{3,2,1,0:T(8,128)S(1)} custom-call(bf16[2,12,2,8,128]{4,3,2,1,0:T(8,128)(2,1)} %bitcast.2, bf16[24]{0:T(256)(128)(2,1)} %eng.1, s32[16]{0:T(128)} %slot_atom_in.1, f32[1,2,8,128]{3,2,1,0:T(8,128)} %pot.1, f32[2,8,128]{2,1,0:T(8,128)} %locp.1, f32[16,128]{1,0:T(8,128)} %beta_in.1, s32[16,128]{1,0:T(8,128)} %support_in.1, ...), custom_call_target="tpu_custom_call" | custom-call | tf_op jit(solution)/shard_map/pallas_call | solution.py:248
  15.8 0.6 %copy.10 = f32[1,2,8,128]{3,2,1,0:T(8,128)} copy(f32[1,2,8,128]{3,2,1,0:T(8,128)S(1)} %shard_map.82) | data formatting | bytes 16384

commit v3 on v2

--- a/solution.py
+++ b/solution.py
@@ -40,9 +40,6 @@
         pltpu.make_async_copy(src, dst, in_sems.at[i]) for i, (src, dst) in enumerate((
             (support_in, support), (beta_in, beta), (slot_atom_in, slot_atom),
             (dcoef_in, dcoef), (pot.at[0], pack_buf.at[k, 0]), (locp, pack_buf.at[k, 1])))]
-    for load in loads:
-        load.start()
-
     barrier = pltpu.get_barrier_semaphore()
     for j in range(1, n):
         pl.semaphore_signal(
@@ -54,6 +51,8 @@
             pl.semaphore_signal(
                 barrier, inc=1, device_id=(before, lax.rem(k + j, n)), device_id_type=MESH)
 
+    for load in loads:
+        load.start()
     pl.semaphore_wait(barrier, n - 1 + half)
 
     def psi_copy(j):
@@ -127,17 +126,16 @@
     if up > u:
         psi32[u * rows:, :] = jnp.zeros(((up - u) * rows, gx), jnp.float32)
     strength = dcoef[...]
-    strength = jnp.concatenate([strength, strength], axis=1)
-    atom_ids = lax.rem(lax.broadcasted_iota(jnp.int32, (2 * atoms, gx), 0), atoms).astype(jnp.float32)
+    atom_ids = lax.broadcasted_iota(jnp.int32, (atoms, gx), 0).astype(jnp.float32)
 
     def project(z, tiles):
         pairs = [split2(tile) for tile in tiles]
         high = jnp.concatenate([p[0] for p in pairs], axis=1)
         low = jnp.concatenate([p[1] for p in pairs], axis=1)
         both = jnp.concatenate([high, low], axis=0)
-        return nt_dot(both, onehot[z])
-
-    proj = jnp.zeros((2 * up, 2 * atoms), jnp.float32)
+        return nt_dot(both, onehot[z, :atoms])
+
+    proj = jnp.zeros((2 * up, atoms), jnp.float32)
     for j in range(n):
         if j == 0:
             @pl.when(jnp.logical_not(takes_prior))
@@ -176,30 +174,30 @@
                 hinv[z, y] = inv
                 x0[z, y] = start
                 state_a[z + 1, y] = start
-                onehot[z, :, y * gx:(y + 1) * gx] = jnp.where(
-                    atom_ids == at, 1.0, 0.0).astype(jnp.bfloat16)
+                hit = jnp.where(atom_ids == at, 1.0, 0.0).astype(jnp.bfloat16)
+                onehot[z, :atoms, y * gx:(y + 1) * gx] = hit
+                onehot[z, atoms:, y * gx:(y + 1) * gx] = hit
                 scaled.append(start * bv)
             proj = proj + project(z, scaled)
 
-    lanes = lax.broadcasted_iota(jnp.int32, (up, 2 * atoms), 1)
     for step in range(ITERS):
         src, dst = (state_a, state_b) if step % 2 == 0 else (state_b, state_a)
         last = step == ITERS - 1
         coefs = (proj[:up] + proj[up:]) * strength
-        high = coefs.astype(jnp.bfloat16).astype(jnp.float32)
-        coefs = jnp.where(lanes < atoms, high, coefs - high).astype(jnp.bfloat16)
-        proj = jnp.zeros((2 * up, 2 * atoms), jnp.float32)
+        coefs = jnp.concatenate(split2(coefs), axis=1)
+        proj = jnp.zeros((2 * up, atoms), jnp.float32)
         for j in list(range(1, n)) + [0]:
             slab = lax.rem(k + j, n) if last else j
             for p in range(planes):
                 z = slab * planes + p
                 back = jnp.dot(coefs, onehot[z], preferred_element_type=jnp.float32)
+                plane = [src[z + 1, y] for y in range(gy)]
                 scaled, sums = [], []
                 for y in range(gy):
                     bv = pack_buf[slab, 2, p, y:y + 1, :]
-                    old = src[z + 1, y]
+                    old = plane[y]
                     near = (src[z, y] + src[z + 2, y]
-                            + src[z + 1, (y + 1) % gy] + src[z + 1, (y - 1) % gy]
+                            + plane[(y + 1) % gy] + plane[(y - 1) % gy]
                             + pltpu.roll(old, 1, 1) + pltpu.roll(old, gx - 1, 1))
                     change = 0.25 * near - (0.5 * bv) * back[:, y * gx:(y + 1) * gx]
                     new = 0.5 * (old + x0[z, y]) + hinv[z, y] * change
@@ -215,6 +213,15 @@
             if last and j > 0:
                 part_copy(j).start()
 
+    for j in range(1, n):
+        psi_copy(j).wait_send()
+        pack_copy(j).wait_send()
+
+    @pl.when(takes_prior)
+    def _():
+        psi_copy(0).wait_send()
+        e_copy.wait_send()
+
     total = part[k]
     for j in range(1, n):
         part_copy(j).wait_recv()
@@ -222,14 +229,7 @@
     out[...] = total.reshape(out.shape)
 
     for j in range(1, n):
-        psi_copy(j).wait_send()
-        pack_copy(j).wait_send()
         part_copy(j).wait_send()
-
-    @pl.when(takes_prior)
-    def _():
-        psi_copy(0).wait_send()
-        e_copy.wait_send()
 
 
 def shards(orbitals, energies, trial_potential, local_potential, beta, support, slot_atom, dcoef):

time: 16.6 us -> 16.3 us (0.982)
  Pallas kernels: 15.8 us -> 15.5 us
    pallas_call x1, Pallas kernels: 15.8 us -> 15.5 us  [shards(): pl.pallas_call(functools.partial(kernel, (n, nb, u, up, planes, gy, gx, a...]
where the time goes in v3:
time: 16.3 us; the launch traced here: 16.1 us
  Pallas kernels  15.5 us (95%)
  local copies, waits for them, and re-layouts  0.6 us (4%)
    pallas_call x1, Pallas kernels, shards(): pl.pallas_call(functools.partial(kernel, (n, nb, u, up, planes, gy, gx, a...  15.5 us
    unnamed x1, local copies, waits for them, and re-layouts  0.6 us

profile of v3, /device:TPU:0, one launch (start us, length us, event | category | flops | bytes accessed | tf_op | source)
XLA Modules:
  0.0 16.1 jit_solution(15174794428019302120)
XLA Ops:
  0.0 15.5 %shard_map.82 = f32[1,2,8,128]{3,2,1,0:T(8,128)S(1)} custom-call(bf16[2,12,2,8,128]{4,3,2,1,0:T(8,128)(2,1)} %bitcast.2, bf16[24]{0:T(256)(128)(2,1)} %eng.1, s32[16]{0:T(128)} %slot_atom_in.1, f32[1,2,8,128]{3,2,1,0:T(8,128)} %pot.1, f32[2,8,128]{2,1,0:T(8,128)} %locp.1, f32[16,128]{1,0:T(8,128)} %beta_in.1, s32[16,128]{1,0:T(8,128)} %support_in.1, ...), custom_call_target="tpu_custom_call" | custom-call | tf_op jit(solution)/shard_map/pallas_call | solution.py:248
  15.5 0.6 %copy.10 = f32[1,2,8,128]{3,2,1,0:T(8,128)} copy(f32[1,2,8,128]{3,2,1,0:T(8,128)S(1)} %shard_map.82) | data formatting | bytes 16384
